TPU v7x, 32 devices: a whole 2x2x4 slice. The times are simulated.
32 devices in a mesh: ctx: 8 (over z, x), fsdp: 4 (over y, core).
Axes of the slice: x: 2, y: 2, z: 4, core: 2. Of those that a mesh axis runs over, the one named last changes fastest.
Arguments:
- inputs: bfloat16 [4, 1024, 768], P('fsdp', 'ctx'), may hold values from -6 to 6
- block_order: int32 [16], replicated, may hold values from 0 to 15, each once
- cotangent: bfloat16 [4, 1024, 768], P('fsdp', 'ctx'), may hold values from -6 to 6
- first_gain: bfloat16 [768], P('fsdp'), may hold values from 0.25 to 1.75
- first_shift: bfloat16 [768], P('fsdp'), may hold values from -3 to 3
- qkv_weight: bfloat16 [768, 2304], P('fsdp')
- qv_bias: bfloat16 [1536], P('fsdp'), may hold values from -3 to 3
- proj_weight: bfloat16 [768, 768], P('fsdp'), may hold values from -1.75 to 1.75
- proj_bias: bfloat16 [768], P('fsdp'), may hold values from -3 to 3
- second_gain: bfloat16 [768], P('fsdp'), may hold values from 0.25 to 1.75
- second_shift: bfloat16 [768], P('fsdp'), may hold values from -3 to 3
- fc_weight: bfloat16 [768, 3072], P('fsdp'), may hold values from -0.21875 to 0.21875
- fc_bias: bfloat16 [3072], P('fsdp'), may hold values from -3 to 3
- down_weight: bfloat16 [3072, 768], P('fsdp'), may hold values from -0.109375 to 0.109375
- down_bias: bfloat16 [768], P('fsdp'), may hold values from -3 to 3
Outputs:
- block_out: bfloat16 [4, 1024, 768], P('fsdp', 'ctx')
- grad_input: float32 [4, 1024, 768], P('fsdp', 'ctx')
- grad_first_gain: float32 [768], P(('ctx', 'fsdp'))
- grad_first_shift: float32 [768], P(('ctx', 'fsdp'))
- grad_qkv_weight: float32 [768, 2304], P('fsdp', 'ctx')
- grad_qv_bias: float32 [1536], P(('ctx', 'fsdp'))
- grad_proj_weight: float32 [768, 768], P('fsdp', 'ctx')
- grad_proj_bias: float32 [768], P(('ctx', 'fsdp'))
- grad_second_gain: float32 [768], P(('ctx', 'fsdp'))
- grad_second_shift: float32 [768], P(('ctx', 'fsdp'))
- grad_fc_weight: float32 [768, 3072], P('fsdp', 'ctx')
- grad_fc_bias: float32 [3072], P(('ctx', 'fsdp'))
- grad_down_weight: float32 [3072, 768], P('fsdp', 'ctx')
- grad_down_bias: float32 [768], P(('ctx', 'fsdp'))
Inputs may be any that keep to these rules, and one draw needn't show every extreme that they name: `block_order`: a permutation of 0 to 15.
All inputs are finite; a program needn't handle non-finite values.
Results may differ from a plain program's by a relative error of at most 0.033.
Values may be sent and summed in bfloat16 or wider, within the bound.
No kernel may reach another device: no remote copies, remote signals or barrier semaphores. Data moves between devices by JAX's collectives and lax.ppermute only.
A program may use at most 256 MiB of HBM per device.

v0:
```python
import math
import jax
import jax.numpy as jnp
from jax import lax
from jax.sharding import PartitionSpec as P

H = 12
HD = 64
epsilon = 1e-05
negative_big = -1e30
gelu_coeff = 0.7978845608028654


def from_behind(value, axis, steps):
    count = lax.axis_size(axis)
    pairs = [(source, (source + steps) % count) for source in range(count)]
    return lax.ppermute(value, axis, pairs)


def split_heads(matrix):
    return matrix.reshape(matrix.shape[0], H, HD)


def norm_forward(rows_in, norm_gain, norm_shift):
    center = rows_in - jnp.mean(rows_in, axis=-1, keepdims=True)
    inverse = lax.rsqrt(jnp.mean(center * center, axis=-1, keepdims=True) + epsilon)
    normed = center * inverse
    return (normed, inverse, (normed * norm_gain + norm_shift).astype(jnp.bfloat16))


def norm_backward(grad_out, normed, inverse, norm_gain):
    scaled = grad_out * norm_gain
    return inverse * (
        scaled
        - jnp.mean(scaled, axis=-1, keepdims=True)
        - normed * jnp.mean(scaled * normed, axis=-1, keepdims=True)
    )


def gelu_pair(hidden_pre):
    argument = gelu_coeff * (hidden_pre + 0.044715 * hidden_pre * hidden_pre * hidden_pre)
    tangent = jnp.tanh(argument)
    result = 0.5 * hidden_pre * (1.0 + tangent)
    derivative = 0.5 * (1.0 + tangent) + 0.5 * hidden_pre * (
        1.0 - tangent * tangent
    ) * gelu_coeff * (1.0 + 3.0 * 0.044715 * hidden_pre * hidden_pre)
    return (result, derivative)


def times_transposed(left_side, right_side):
    return lax.dot_general(
        left_side, right_side, (((1,), (1,)), ((), ())), preferred_element_type=jnp.float32
    )


def transposed_times(left_side, right_side):
    return lax.dot_general(
        left_side, right_side, (((0,), (0,)), ((), ())), preferred_element_type=jnp.float32
    )


def positions_of(block_order, first_row, row_count, block_rows):
    row_ids = first_row + jnp.arange(row_count, dtype=jnp.int32)
    owners = row_ids // block_rows
    matches = owners[:, None] == jnp.arange(block_order.shape[0], dtype=jnp.int32)[None, :]
    blocks = jnp.sum(jnp.where(matches, block_order[None, :], 0), axis=1)
    return blocks * block_rows + row_ids % block_rows


def head_scores(queries, key_rows):
    return jnp.einsum(
        "qhd,khd->hqk",
        split_heads(queries),
        split_heads(key_rows),
        preferred_element_type=jnp.float32,
    ) * (1.0 / math.sqrt(HD))


def attend_block(carry, queries, key_rows, values, visible):

    def attend_compute(running):
        run_max, run_sum, accumulated = running
        scores = jnp.where(visible[None], head_scores(queries, key_rows), negative_big)
        new_max = jnp.maximum(run_max, jnp.max(scores, axis=2))
        weights = jnp.where(visible[None], jnp.exp(scores - new_max[:, :, None]), 0.0)
        factor = jnp.exp(run_max - new_max)
        mixed = jnp.einsum(
            "hqk,khd->qhd",
            weights.astype(jnp.bfloat16),
            split_heads(values),
            preferred_element_type=jnp.float32,
        )
        return (new_max, jnp.sum(weights, axis=2), accumulated * factor.T[:, :, None] + mixed)

    return lax.cond(jnp.any(visible), attend_compute, lambda running: running, carry)


def softmax_grads(queries, key_rows, values, attended_grad, lse_rows, delta_rows, visible):
    probs = jnp.where(
        visible[None], jnp.exp(head_scores(queries, key_rows) - lse_rows.T[:, :, None]), 0.0
    )
    prob_grad = jnp.einsum(
        "qhd,khd->hqk",
        split_heads(attended_grad),
        split_heads(values),
        preferred_element_type=jnp.float32,
    )
    score_grad = (probs * (prob_grad - delta_rows.T[:, :, None])).astype(jnp.bfloat16)
    return (probs, score_grad)


def both_block(carry, queries, key_rows, values, attended_grad, lse_rows, delta_rows, visible):

    def both_compute(totals):
        probs, score_grad = softmax_grads(
            queries, key_rows, values, attended_grad, lse_rows, delta_rows, visible
        )
        scale_factor = 1.0 / math.sqrt(HD)
        query_total = (
            totals[0]
            + jnp.einsum(
                "hqk,khd->qhd",
                score_grad,
                split_heads(key_rows),
                preferred_element_type=jnp.float32,
            )
            * scale_factor
        )
        key_total = (
            totals[1]
            + jnp.einsum(
                "hqk,qhd->khd", score_grad, split_heads(queries), preferred_element_type=jnp.float32
            )
            * scale_factor
        )
        value_total = totals[2] + jnp.einsum(
            "hqk,qhd->khd",
            probs.astype(jnp.bfloat16),
            split_heads(attended_grad),
            preferred_element_type=jnp.float32,
        )
        return (query_total, key_total, value_total)

    return lax.cond(jnp.any(visible), both_compute, lambda totals: totals, carry)


def on_device(
    inputs,
    block_order,
    cotangent,
    first_gain,
    first_shift,
    qkv_weight,
    qv_bias,
    proj_weight,
    proj_bias,
    second_gain,
    second_shift,
    fc_weight,
    fc_bias,
    down_weight,
    down_bias,
):
    (
        first_gain,
        first_shift,
        qkv_weight,
        qv_bias,
        proj_weight,
        proj_bias,
        second_gain,
        second_shift,
        fc_weight,
        fc_bias,
        down_weight,
        down_bias,
    ) = (
        lax.all_gather(first_gain, "fsdp", axis=0, tiled=True),
        lax.all_gather(first_shift, "fsdp", axis=0, tiled=True),
        lax.all_gather(qkv_weight, "fsdp", axis=0, tiled=True),
        lax.all_gather(qv_bias, "fsdp", axis=0, tiled=True),
        lax.all_gather(proj_weight, "fsdp", axis=0, tiled=True),
        lax.all_gather(proj_bias, "fsdp", axis=0, tiled=True),
        lax.all_gather(second_gain, "fsdp", axis=0, tiled=True),
        lax.all_gather(second_shift, "fsdp", axis=0, tiled=True),
        lax.all_gather(fc_weight, "fsdp", axis=0, tiled=True),
        lax.all_gather(fc_bias, "fsdp", axis=0, tiled=True),
        lax.all_gather(down_weight, "fsdp", axis=0, tiled=True),
        lax.all_gather(down_bias, "fsdp", axis=0, tiled=True),
    )
    tokens = inputs[0].astype(jnp.float32)
    upstream = cotangent[0]
    rows_dev = tokens.shape[0]
    block_rows = rows_dev // 2
    model_width = tokens.shape[1]
    block_slot = lax.axis_index("ctx")
    own_pos = positions_of(block_order, block_slot * rows_dev, rows_dev, block_rows)
    first_normed, first_inverse, first_hidden = norm_forward(tokens, first_gain, first_shift)
    projected = jnp.dot(first_hidden, qkv_weight, preferred_element_type=jnp.float32)
    queries = (projected[:, :model_width] + qv_bias[:model_width]).astype(jnp.bfloat16)
    key_rows = projected[:, model_width : 2 * model_width].astype(jnp.bfloat16)
    values = (projected[:, 2 * model_width :] + qv_bias[model_width:]).astype(jnp.bfloat16)
    start_state = (
        jnp.full((H, rows_dev), negative_big, jnp.float32),
        jnp.zeros((H, rows_dev), jnp.float32),
        jnp.zeros((rows_dev, H, HD), jnp.float32),
    )
    incoming = (
        lax.all_gather(key_rows, "ctx", axis=0, tiled=True),
        lax.all_gather(values, "ctx", axis=0, tiled=True),
    )
    key_pos = positions_of(block_order, jnp.int32(0), incoming[0].shape[0], block_rows)
    visible = key_pos[None, :] <= own_pos[:, None]
    run_max, run_sum, accumulated = attend_block(
        start_state, queries, incoming[0], incoming[1], visible
    )
    lse_rows = (run_max + jnp.log(run_sum)).T
    attended = (
        (accumulated / run_sum.T[:, :, None]).reshape(rows_dev, model_width).astype(jnp.bfloat16)
    )
    residual = (
        tokens + jnp.dot(attended, proj_weight, preferred_element_type=jnp.float32) + proj_bias
    )
    second_normed, second_inverse, second_hidden = norm_forward(residual, second_gain, second_shift)
    hidden_pre = jnp.dot(second_hidden, fc_weight, preferred_element_type=jnp.float32) + fc_bias
    activation, derivative = gelu_pair(hidden_pre)
    activation_b = activation.astype(jnp.bfloat16)
    block_out = (
        residual
        + jnp.dot(activation_b, down_weight, preferred_element_type=jnp.float32)
        + down_bias
    ).astype(jnp.bfloat16)
    upstream_f = upstream.astype(jnp.float32)
    down_wgrad = transposed_times(activation_b, upstream)
    down_bgrad = jnp.sum(upstream_f, axis=0)
    pre_grad = times_transposed(upstream, down_weight) * derivative
    pre_grad_b = pre_grad.astype(jnp.bfloat16)
    fc_wgrad = transposed_times(second_hidden, pre_grad_b)
    fc_bgrad = jnp.sum(pre_grad, axis=0)
    second_grad = times_transposed(pre_grad_b, fc_weight)
    second_ggrad = jnp.sum(second_grad * second_normed, axis=0)
    second_sgrad = jnp.sum(second_grad, axis=0)
    residual_grad = upstream_f + norm_backward(
        second_grad, second_normed, second_inverse, second_gain
    )
    residual_grad_b = residual_grad.astype(jnp.bfloat16)
    proj_wgrad = transposed_times(attended, residual_grad_b)
    proj_bgrad = jnp.sum(residual_grad, axis=0)
    attended_grad = times_transposed(residual_grad_b, proj_weight).astype(jnp.bfloat16)
    delta_rows = jnp.einsum(
        "qhd,qhd->qh",
        split_heads(attended_grad),
        split_heads(attended),
        preferred_element_type=jnp.float32,
    )
    zero_heads = jnp.zeros((rows_dev, H, HD), jnp.float32)
    cycle_count = lax.axis_size("ctx")

    def cycle_step(step_index, state):
        held_keys, held_values, query_total, key_total, value_total = state
        anchor = (block_slot - step_index) % cycle_count
        key_pos = positions_of(block_order, anchor * rows_dev, rows_dev, block_rows)
        visible = key_pos[None, :] <= own_pos[:, None]
        query_total, key_total, value_total = both_block(
            (query_total, key_total, value_total),
            queries,
            held_keys,
            held_values,
            attended_grad,
            lse_rows,
            delta_rows,
            visible,
        )
        held_keys, held_values, key_total, value_total = (
            from_behind(held_keys, "ctx", 1),
            from_behind(held_values, "ctx", 1),
            from_behind(key_total.astype(jnp.bfloat16), "ctx", 1).astype(key_total.dtype),
            from_behind(value_total.astype(jnp.bfloat16), "ctx", 1).astype(value_total.dtype),
        )
        return (held_keys, held_values, query_total, key_total, value_total)

    start_cycle = (key_rows, values, zero_heads, zero_heads, zero_heads)
    unused_keys, unused_values, query_grad, key_grad, value_grad = lax.fori_loop(
        0, cycle_count, cycle_step, start_cycle
    )
    query_grad = query_grad.reshape(rows_dev, model_width)
    key_grad = key_grad.reshape(rows_dev, model_width)
    value_grad = value_grad.reshape(rows_dev, model_width)
    qkv_grad = jnp.concatenate([query_grad, key_grad, value_grad], axis=1).astype(jnp.bfloat16)
    qkv_wgrad = transposed_times(first_hidden, qkv_grad)
    qv_bgrad = jnp.concatenate([jnp.sum(query_grad, axis=0), jnp.sum(value_grad, axis=0)])
    first_grad = times_transposed(qkv_grad, qkv_weight)
    first_ggrad = jnp.sum(first_grad * first_normed, axis=0)
    first_sgrad = jnp.sum(first_grad, axis=0)
    input_grad = residual_grad + norm_backward(first_grad, first_normed, first_inverse, first_gain)
    vector_terms = (
        first_ggrad,
        first_sgrad,
        qv_bgrad,
        proj_bgrad,
        second_ggrad,
        second_sgrad,
        fc_bgrad,
        down_bgrad,
    )
    vector_sums = (
        lax.psum_scatter(vector_terms[0], ("ctx", "fsdp"), scatter_dimension=0, tiled=True),
        lax.psum_scatter(vector_terms[1], ("ctx", "fsdp"), scatter_dimension=0, tiled=True),
        lax.psum_scatter(vector_terms[2], ("ctx", "fsdp"), scatter_dimension=0, tiled=True),
        lax.psum_scatter(vector_terms[3], ("ctx", "fsdp"), scatter_dimension=0, tiled=True),
        lax.psum_scatter(vector_terms[4], ("ctx", "fsdp"), scatter_dimension=0, tiled=True),
        lax.psum_scatter(vector_terms[5], ("ctx", "fsdp"), scatter_dimension=0, tiled=True),
        lax.psum_scatter(vector_terms[6], ("ctx", "fsdp"), scatter_dimension=0, tiled=True),
        lax.psum_scatter(vector_terms[7], ("ctx", "fsdp"), scatter_dimension=0, tiled=True),
    )
    matrix_terms = (qkv_wgrad, proj_wgrad, fc_wgrad, down_wgrad)
    row_sums = (
        lax.psum_scatter(
            matrix_terms[0].astype(jnp.bfloat16), "fsdp", scatter_dimension=0, tiled=True
        ).astype(jnp.float32),
        lax.psum_scatter(
            matrix_terms[1].astype(jnp.bfloat16), "fsdp", scatter_dimension=0, tiled=True
        ).astype(jnp.float32),
        lax.psum_scatter(
            matrix_terms[2].astype(jnp.bfloat16), "fsdp", scatter_dimension=0, tiled=True
        ).astype(jnp.float32),
        lax.psum_scatter(
            matrix_terms[3].astype(jnp.bfloat16), "fsdp", scatter_dimension=0, tiled=True
        ).astype(jnp.float32),
    )
    matrix_sums = (
        lax.psum_scatter(row_sums[0], "ctx", scatter_dimension=1, tiled=True),
        lax.psum_scatter(row_sums[1], "ctx", scatter_dimension=1, tiled=True),
        lax.psum_scatter(row_sums[2], "ctx", scatter_dimension=1, tiled=True),
        lax.psum_scatter(row_sums[3], "ctx", scatter_dimension=1, tiled=True),
    )
    return (
        block_out[None],
        input_grad[None],
        vector_sums[0],
        vector_sums[1],
        matrix_sums[0],
        vector_sums[2],
        matrix_sums[1],
        vector_sums[3],
        vector_sums[4],
        vector_sums[5],
        matrix_sums[2],
        vector_sums[6],
        matrix_sums[3],
        vector_sums[7],
    )


def solution(mesh):
    placed = (
        P("fsdp", "ctx", None),
        P(),
        P("fsdp", "ctx", None),
        P("fsdp"),
        P("fsdp"),
        P("fsdp", None),
        P("fsdp"),
        P("fsdp", None),
        P("fsdp"),
        P("fsdp"),
        P("fsdp"),
        P("fsdp", None),
        P("fsdp"),
        P("fsdp", None),
        P("fsdp"),
    )
    return jax.shard_map(
        on_device,
        mesh=mesh,
        in_specs=placed,
        out_specs=(
            P("fsdp", "ctx", None),
            P("fsdp", "ctx", None),
            P(("ctx", "fsdp")),
            P(("ctx", "fsdp")),
            P("fsdp", "ctx"),
            P(("ctx", "fsdp")),
            P("fsdp", "ctx"),
            P(("ctx", "fsdp")),
            P(("ctx", "fsdp")),
            P(("ctx", "fsdp")),
            P("fsdp", "ctx"),
            P(("ctx", "fsdp")),
            P("fsdp", "ctx"),
            P(("ctx", "fsdp")),
        ),
        check_vma=False,
    )
```

profile of v0, /device:TPU:0, one launch (start us, length us, event | category | flops | bytes accessed | tf_op | source)
XLA Modules:
  0.0 852.1 jit_solution(7596826350199663733)
XLA Ops:
  14.9 14.1 %all-reduce.15 = (bf16[768]{0:T(1024)(128)(2,1)S(1)}, bf16[768]{0:T(1024)(128)(2,1)S(1)}, bf16[768]{0:T(1024)(128)(2,1)S(1)}, bf16[768]{0:T(1024)(128)(2,1)S(1)}...) all-reduce(bf16[768]{0:T(1024)(128)(2,1)S(1)} %dynamic-update-slice, ...), channel_id=1, replica_groups=mesh['ctx'=8,'fsdp'=4] {'fsdp'}, use_global_device_ids=true, to_apply=%add.1 | all-reduce | flops 4608 | bytes 18432
  31.2 12.0 %all-gather.9.cloned.1.call-done = bf16[768,2304]{1,0:T(8,128)(2,1)} async-done(((bf16[192,2304]{1,0:T(8,128)(2,1)}), bf16[768,2304]{1,0:T(8,128)(2,1)}) %all-gather.9.cloned.1.call-update) | async-done | bytes 3538960 | tf_op jit(solution)/shard_map/all_gather | solution.py:180
  46.8 5.2 all-gather
  57.6 5.2 all-gather.1
  63.9 27.2 %all-gather.11.cloned.1.call-done = bf16[1024,768]{1,0:T(8,128)(2,1)} async-done(((bf16[128,768]{1,0:T(8,128)(2,1)}), bf16[1024,768]{1,0:T(8,128)(2,1)}) %all-gather.11.cloned.1.call-update) | async-done | bytes 1572880 | tf_op jit(solution)/shard_map/all_gather | solution.py:209
  91.1 45.3 %all-gather.13.cloned.1.call-done = bf16[1024,768]{1,0:T(8,128)(2,1)} async-done(((bf16[128,768]{1,0:T(8,128)(2,1)}), bf16[1024,768]{1,0:T(8,128)(2,1)}) %all-gather.13.cloned.1.call-update) | async-done | bytes 1572880 | tf_op jit(solution)/shard_map/all_gather | solution.py:210
  136.4 13.5 %conditional.2 = (f32[12,128]{1,0:T(8,128)S(1)}, f32[12,128]{1,0:T(8,128)S(1)}, f32[128,12,64]{0,2,1:T(8,128)S(1)}, f32[12,128]{1,0:T(8,128)S(1)}) conditional(s32[]{:T(128)} %convert_element_type.167, () %tuple.50, (pred[128,1024]{1,0:T(8,128)(4,1)}, bf16[128,768]{1,0:T(8,128)(2,1)S(1)}, bf16[1024,768]{1,0:T(8,128)(2,1)}, ...), branch_computations={%region_5.6_spmd, %region_6.9_spmd} | conditional | flops 423200256 | bytes 61829348 | solution.py:95
  144.6 5.1 fusion.9
  156.2 36.4 %all-gather.17.cloned.1.call-done = bf16[768,3072]{1,0:T(8,128)(2,1)} async-done(((bf16[192,3072]{1,0:T(8,128)(2,1)}), bf16[768,3072]{1,0:T(8,128)(2,1)}) %all-gather.17.cloned.1.call-update) | async-done | bytes 4718608 | tf_op jit(solution)/shard_map/all_gather | solution.py:186
  195.8 35.6 %all-gather.19.cloned.1.call-done = bf16[3072,768]{1,0:T(8,128)(2,1)} async-done(((bf16[768,768]{1,0:T(8,128)(2,1)}), bf16[3072,768]{1,0:T(8,128)(2,1)}) %all-gather.19.cloned.1.call-update) | async-done | bytes 4718608 | tf_op jit(solution)/shard_map/all_gather | solution.py:188
  231.5 5.0 fusion.85
  244.9 174.3 %while.25 = (s32[]{:T(128)}, bf16[128,768]{0,1:T(8,128)(2,1)S(1)}, bf16[128,768]{0,1:T(8,128)(2,1)S(1)}, f32[128,12,64]{0,2,1:T(8,128)S(1)}, f32[128,12,64]{0,2,...) while((s32[]{:T(128)}, bf16[128,768]{0,1:T(8,128)(2,1)S(1)}, ...), condition=%wide.region_18.19_spmd.clone, body=%wide.region_13.18_spmd.clone.sunk | while | flops 128329360 | bytes 15188138 | solution.py:283
  254.4 4.5 collective-permute-done.2
  258.9 4.2 collective-permute-done.3
  263.1 4.2 collective-permute-done
  276.7 6.3 collective-permute-done.2
  283.0 4.2 collective-permute-done.3
  287.2 4.2 collective-permute-done
  299.9 8.1 collective-permute-done.2
  321.2 9.2 %collective-permute-done.2 = bf16[128,12,64]{0,2,1:T(8,128)(2,1)S(1)} collective-permute-done((bf16[128,12,64]{0,2,1:T(8,128)(2,1)S(1)}, bf16[128,12,64]{0,2,1:T(8,128)(2,1)S(1)}, u32[]{:S(2)}, u32[]{:S(2)}) %collective-permute-start.2) | collective-permute-done | bytes 196640 | tf_op jit(solution)/shard_map/while/body/eval_jaxpr/ppermute | solution.py:17
  343.2 8.7 %collective-permute-done.2 = bf16[128,12,64]{0,2,1:T(8,128)(2,1)S(1)} collective-permute-done((bf16[128,12,64]{0,2,1:T(8,128)(2,1)S(1)}, bf16[128,12,64]{0,2,1:T(8,128)(2,1)S(1)}, u32[]{:S(2)}, u32[]{:S(2)}) %collective-permute-start.2) | collective-permute-done | bytes 196640 | tf_op jit(solution)/shard_map/while/body/eval_jaxpr/ppermute | solution.py:17
  365.2 7.5 collective-permute-done.2
  386.2 8.1 collective-permute-done.2
  406.4 6.5 collective-permute-done.2
  435.5 25.0 %reduce-scatter.15.cloned.1.call-done = bf16[192,2304]{1,0:T(8,128)(2,1)} async-done(((bf16[768,2304]{1,0:T(8,128)(2,1)}), bf16[192,2304]{1,0:T(8,128)(2,1)}) %reduce-scatter.15.cloned.1.call-update) | async-done | bytes 884752 | tf_op jit(solution)/shard_map/reduce_scatter | solution.py:318
  463.3 47.8 %reduce-scatter.19.cloned.1.call-done = bf16[192,3072]{1,0:T(8,128)(2,1)} async-done(((bf16[768,3072]{1,0:T(8,128)(2,1)}), bf16[192,3072]{1,0:T(8,128)(2,1)}) %reduce-scatter.19.cloned.1.call-update) | async-done | bytes 1179664 | tf_op jit(solution)/shard_map/reduce_scatter | solution.py:324
  514.1 47.4 %reduce-scatter.23.cloned.1.call-done = bf16[768,768]{1,0:T(8,128)(2,1)} async-done(((bf16[3072,768]{1,0:T(8,128)(2,1)}), bf16[768,768]{1,0:T(8,128)(2,1)}) %reduce-scatter.23.cloned.1.call-update) | async-done | bytes 1179664 | tf_op jit(solution)/shard_map/reduce_scatter | solution.py:327
  569.7 40.5 %all-reduce.14 = (f32[768]{0:T(1024)S(1)}, f32[768]{0:T(1024)S(1)}, f32[1536]{0:T(1024)S(1)}, f32[768]{0:T(1024)S(1)}, f32[768]{0:T(1024)S(1)}, /*index=5*/f32[7...) all-reduce(f32[768]{0:T(1024)} %get-tuple-element.608, ...), channel_id=2, replica_groups=mesh['ctx'=8,'fsdp'=4] {'ctx','fsdp'}, use_global_device_ids=true, to_apply=%region_22.23.clone | all-reduce | flops 9216 | bytes 73728
  621.7 6.4 reduce-scatter.27.cloned.1.call-done
  629.7 70.3 %reduce-scatter.25.cloned.1.call-done = f32[288,192]{1,0:T(8,128)} async-done(((f32[2304,192]{1,0:T(8,128)}), f32[288,192]{1,0:T(8,128)}) %reduce-scatter.25.cloned.1.call-update) | async-done | bytes 221200
  701.9 71.0 %reduce-scatter.21.cloned.1.call-done = f32[192,384]{1,0:T(8,128)} async-done(((f32[192,3072]{1,0:T(8,128)}), f32[192,384]{1,0:T(8,128)}) %reduce-scatter.21.cloned.1.call-update) | async-done | bytes 294928 | tf_op jit(solution)/shard_map/reduce_scatter | solution.py:334
  772.9 72.7 %reduce-scatter.29.cloned.1.call-done = f32[96,768]{1,0:T(8,128)} async-done(((f32[768,768]{1,0:T(8,128)}), f32[96,768]{1,0:T(8,128)}) %reduce-scatter.29.cloned.1.call-update) | async-done | bytes 294928
  (377 shorter events, 187.6 us)
Async XLA Ops:
  7.2 36.0 %all-gather.9.cloned.1.call-start = ((), (), s32[]{:S(2)}) async-start(), calls=%async_computation.8 | async-start | bytes 4423680 | tf_op jit(solution)/shard_map/all_gather | solution.py:180
  7.9 83.2 %all-gather.11.cloned.1.call-start = ((), (), s32[]{:S(2)}) async-start(), calls=%async_computation.9 | async-start | bytes 1769472 | tf_op jit(solution)/shard_map/all_gather | solution.py:209
  46.8 89.7 %all-gather.13.cloned.1.call-start = ((), (), s32[]{:S(2)}) async-start(), calls=%async_computation.10 | async-start | bytes 1769472 | tf_op jit(solution)/shard_map/all_gather | solution.py:210
  52.8 100.9 %all-gather.15.cloned.1.call-start = ((), (), s32[]{:S(2)}) async-start(), calls=%async_computation.11 | async-start | bytes 1474560 | tf_op jit(solution)/shard_map/all_gather | solution.py:182
  53.4 139.1 %all-gather.17.cloned.1.call-start = ((), (), s32[]{:S(2)}) async-start(), calls=%async_computation.12 | async-start | bytes 5898240 | tf_op jit(solution)/shard_map/all_gather | solution.py:186
  54.0 177.4 %all-gather.19.cloned.1.call-start = ((), (), s32[]{:S(2)}) async-start(), calls=%async_computation.13 | async-start | bytes 5898240 | tf_op jit(solution)/shard_map/all_gather | solution.py:188
  54.6 378.8 %reduce-scatter.17.cloned.1.call-start = ((), (), s32[]{:S(2)}) async-start(), calls=%async_computation.15 | async-start | bytes 1474560 | tf_op jit(solution)/shard_map/reduce_scatter | solution.py:321
  244.7 215.8 %reduce-scatter.15.cloned.1.call-start = ((), (), s32[]{:S(2)}) async-start(), calls=%async_computation.14 | async-start | bytes 4423680 | tf_op jit(solution)/shard_map/reduce_scatter | solution.py:318
  251.4 15.9 %collective-permute-start = (bf16[128,768]{0,1:T(8,128)(2,1)S(1)}, bf16[128,768]{0,1:T(8,128)(2,1)S(1)}, u32[]{:S(2)}, u32[]{:S(2)}) collective-permute-start(bf16[128,768]{0,1:T(8,128)(2,1)S(1)} %copy.103), channel_id=1, source_target_pairs={{0,4},{4,8},{8,12},{12,16},{16,20},{20,24},{24,28},{28,0},{1,5},{5... | collective-permute-start | bytes 589832 | tf_op jit(solution)/shard_map/while/body/eval_jaxpr/ppermute | solution.py:17
  252.9 17.9 %collective-permute-start.1 = (bf16[128,768]{0,1:T(8,128)(2,1)S(1)}, bf16[128,768]{0,1:T(8,128)(2,1)S(1)}, u32[]{:S(2)}, u32[]{:S(2)}) collective-permute-start(bf16[128,768]{0,1:T(8,128)(2,1)S(1)} %copy.104), channel_id=1, source_target_pairs={{0,4},{4,8},{8,12},{12,16},{16,20},{20,24},{24,28},{28,0},{1,5},{5... | collective-permute-start | bytes 589832 | tf_op jit(solution)/shard_map/while/body/eval_jaxpr/ppermute | solution.py:17
  275.5 15.9 %collective-permute-start = (bf16[128,768]{0,1:T(8,128)(2,1)S(1)}, bf16[128,768]{0,1:T(8,128)(2,1)S(1)}, u32[]{:S(2)}, u32[]{:S(2)}) collective-permute-start(bf16[128,768]{0,1:T(8,128)(2,1)S(1)} %copy.103), channel_id=1, source_target_pairs={{0,4},{4,8},{8,12},{12,16},{16,20},{20,24},{24,28},{28,0},{1,5},{5... | collective-permute-start | bytes 589832 | tf_op jit(solution)/shard_map/while/body/eval_jaxpr/ppermute | solution.py:17
  276.1 18.0 %collective-permute-start.1 = (bf16[128,768]{0,1:T(8,128)(2,1)S(1)}, bf16[128,768]{0,1:T(8,128)(2,1)S(1)}, u32[]{:S(2)}, u32[]{:S(2)}) collective-permute-start(bf16[128,768]{0,1:T(8,128)(2,1)S(1)} %copy.104), channel_id=1, source_target_pairs={{0,4},{4,8},{8,12},{12,16},{16,20},{20,24},{24,28},{28,0},{1,5},{5... | collective-permute-start | bytes 589832 | tf_op jit(solution)/shard_map/while/body/eval_jaxpr/ppermute | solution.py:17
  297.6 14.6 %collective-permute-start.3 = (bf16[128,12,64]{0,2,1:T(8,128)(2,1)S(1)}, bf16[128,12,64]{0,2,1:T(8,128)(2,1)S(1)}, u32[]{:S(2)}, u32[]{:S(2)}) collective-permute-start(bf16[128,12,64]{0,2,1:T(8,128)(2,1)S(1)} %convert_element_type.301), channel_id=1, source_target_pairs={{0,4},{4,8},{8,12},{12,16},{16,20},{20,24},{24,28},{28,0},{1,5},{5... | collective-permute-start | bytes 589832 | tf_op jit(solution)/shard_map/while/body/eval_jaxpr/ppermute | solution.py:17
  298.7 17.4 %collective-permute-start = (bf16[128,768]{0,1:T(8,128)(2,1)S(1)}, bf16[128,768]{0,1:T(8,128)(2,1)S(1)}, u32[]{:S(2)}, u32[]{:S(2)}) collective-permute-start(bf16[128,768]{0,1:T(8,128)(2,1)S(1)} %copy.103), channel_id=1, source_target_pairs={{0,4},{4,8},{8,12},{12,16},{16,20},{20,24},{24,28},{28,0},{1,5},{5... | collective-permute-start | bytes 589832 | tf_op jit(solution)/shard_map/while/body/eval_jaxpr/ppermute | solution.py:17
  298.8 19.4 %collective-permute-start.1 = (bf16[128,768]{0,1:T(8,128)(2,1)S(1)}, bf16[128,768]{0,1:T(8,128)(2,1)S(1)}, u32[]{:S(2)}, u32[]{:S(2)}) collective-permute-start(bf16[128,768]{0,1:T(8,128)(2,1)S(1)} %copy.104), channel_id=1, source_target_pairs={{0,4},{4,8},{8,12},{12,16},{16,20},{20,24},{24,28},{28,0},{1,5},{5... | collective-permute-start | bytes 589832 | tf_op jit(solution)/shard_map/while/body/eval_jaxpr/ppermute | solution.py:17
  320.0 14.6 %collective-permute-start.3 = (bf16[128,12,64]{0,2,1:T(8,128)(2,1)S(1)}, bf16[128,12,64]{0,2,1:T(8,128)(2,1)S(1)}, u32[]{:S(2)}, u32[]{:S(2)}) collective-permute-start(bf16[128,12,64]{0,2,1:T(8,128)(2,1)S(1)} %convert_element_type.301), channel_id=1, source_target_pairs={{0,4},{4,8},{8,12},{12,16},{16,20},{20,24},{24,28},{28,0},{1,5},{5... | collective-permute-start | bytes 589832 | tf_op jit(solution)/shard_map/while/body/eval_jaxpr/ppermute | solution.py:17
  321.1 16.6 %collective-permute-start = (bf16[128,768]{0,1:T(8,128)(2,1)S(1)}, bf16[128,768]{0,1:T(8,128)(2,1)S(1)}, u32[]{:S(2)}, u32[]{:S(2)}) collective-permute-start(bf16[128,768]{0,1:T(8,128)(2,1)S(1)} %copy.103), channel_id=1, source_target_pairs={{0,4},{4,8},{8,12},{12,16},{16,20},{20,24},{24,28},{28,0},{1,5},{5... | collective-permute-start | bytes 589832 | tf_op jit(solution)/shard_map/while/body/eval_jaxpr/ppermute | solution.py:17
  321.1 18.6 %collective-permute-start.1 = (bf16[128,768]{0,1:T(8,128)(2,1)S(1)}, bf16[128,768]{0,1:T(8,128)(2,1)S(1)}, u32[]{:S(2)}, u32[]{:S(2)}) collective-permute-start(bf16[128,768]{0,1:T(8,128)(2,1)S(1)} %copy.104), channel_id=1, source_target_pairs={{0,4},{4,8},{8,12},{12,16},{16,20},{20,24},{24,28},{28,0},{1,5},{5... | collective-permute-start | bytes 589832 | tf_op jit(solution)/shard_map/while/body/eval_jaxpr/ppermute | solution.py:17
  341.6 14.6 %collective-permute-start.3 = (bf16[128,12,64]{0,2,1:T(8,128)(2,1)S(1)}, bf16[128,12,64]{0,2,1:T(8,128)(2,1)S(1)}, u32[]{:S(2)}, u32[]{:S(2)}) collective-permute-start(bf16[128,12,64]{0,2,1:T(8,128)(2,1)S(1)} %convert_element_type.301), channel_id=1, source_target_pairs={{0,4},{4,8},{8,12},{12,16},{16,20},{20,24},{24,28},{28,0},{1,5},{5... | collective-permute-start | bytes 589832 | tf_op jit(solution)/shard_map/while/body/eval_jaxpr/ppermute | solution.py:17
  342.6 15.8 %collective-permute-start = (bf16[128,768]{0,1:T(8,128)(2,1)S(1)}, bf16[128,768]{0,1:T(8,128)(2,1)S(1)}, u32[]{:S(2)}, u32[]{:S(2)}) collective-permute-start(bf16[128,768]{0,1:T(8,128)(2,1)S(1)} %copy.103), channel_id=1, source_target_pairs={{0,4},{4,8},{8,12},{12,16},{16,20},{20,24},{24,28},{28,0},{1,5},{5... | collective-permute-start | bytes 589832 | tf_op jit(solution)/shard_map/while/body/eval_jaxpr/ppermute | solution.py:17
  342.6 17.8 %collective-permute-start.1 = (bf16[128,768]{0,1:T(8,128)(2,1)S(1)}, bf16[128,768]{0,1:T(8,128)(2,1)S(1)}, u32[]{:S(2)}, u32[]{:S(2)}) collective-permute-start(bf16[128,768]{0,1:T(8,128)(2,1)S(1)} %copy.104), channel_id=1, source_target_pairs={{0,4},{4,8},{8,12},{12,16},{16,20},{20,24},{24,28},{28,0},{1,5},{5... | collective-permute-start | bytes 589832 | tf_op jit(solution)/shard_map/while/body/eval_jaxpr/ppermute | solution.py:17
  363.2 15.0 %collective-permute-start = (bf16[128,768]{0,1:T(8,128)(2,1)S(1)}, bf16[128,768]{0,1:T(8,128)(2,1)S(1)}, u32[]{:S(2)}, u32[]{:S(2)}) collective-permute-start(bf16[128,768]{0,1:T(8,128)(2,1)S(1)} %copy.103), channel_id=1, source_target_pairs={{0,4},{4,8},{8,12},{12,16},{16,20},{20,24},{24,28},{28,0},{1,5},{5... | collective-permute-start | bytes 589832 | tf_op jit(solution)/shard_map/while/body/eval_jaxpr/ppermute | solution.py:17
  363.3 17.0 %collective-permute-start.1 = (bf16[128,768]{0,1:T(8,128)(2,1)S(1)}, bf16[128,768]{0,1:T(8,128)(2,1)S(1)}, u32[]{:S(2)}, u32[]{:S(2)}) collective-permute-start(bf16[128,768]{0,1:T(8,128)(2,1)S(1)} %copy.104), channel_id=1, source_target_pairs={{0,4},{4,8},{8,12},{12,16},{16,20},{20,24},{24,28},{28,0},{1,5},{5... | collective-permute-start | bytes 589832 | tf_op jit(solution)/shard_map/while/body/eval_jaxpr/ppermute | solution.py:17
  383.9 15.0 %collective-permute-start = (bf16[128,768]{0,1:T(8,128)(2,1)S(1)}, bf16[128,768]{0,1:T(8,128)(2,1)S(1)}, u32[]{:S(2)}, u32[]{:S(2)}) collective-permute-start(bf16[128,768]{0,1:T(8,128)(2,1)S(1)} %copy.103), channel_id=1, source_target_pairs={{0,4},{4,8},{8,12},{12,16},{16,20},{20,24},{24,28},{28,0},{1,5},{5... | collective-permute-start | bytes 589832 | tf_op jit(solution)/shard_map/while/body/eval_jaxpr/ppermute | solution.py:17
  384.0 17.1 %collective-permute-start.1 = (bf16[128,768]{0,1:T(8,128)(2,1)S(1)}, bf16[128,768]{0,1:T(8,128)(2,1)S(1)}, u32[]{:S(2)}, u32[]{:S(2)}) collective-permute-start(bf16[128,768]{0,1:T(8,128)(2,1)S(1)} %copy.104), channel_id=1, source_target_pairs={{0,4},{4,8},{8,12},{12,16},{16,20},{20,24},{24,28},{28,0},{1,5},{5... | collective-permute-start | bytes 589832 | tf_op jit(solution)/shard_map/while/body/eval_jaxpr/ppermute | solution.py:17
  403.2 16.0 %collective-permute-start.1 = (bf16[128,768]{0,1:T(8,128)(2,1)S(1)}, bf16[128,768]{0,1:T(8,128)(2,1)S(1)}, u32[]{:S(2)}, u32[]{:S(2)}) collective-permute-start(bf16[128,768]{0,1:T(8,128)(2,1)S(1)} %copy.104), channel_id=1, source_target_pairs={{0,4},{4,8},{8,12},{12,16},{16,20},{20,24},{24,28},{28,0},{1,5},{5... | collective-permute-start | bytes 589832 | tf_op jit(solution)/shard_map/while/body/eval_jaxpr/ppermute | solution.py:17
  422.9 88.2 %reduce-scatter.19.cloned.1.call-start = ((), (), s32[]{:S(2)}) async-start(), calls=%async_computation.16 | async-start | bytes 5898240 | tf_op jit(solution)/shard_map/reduce_scatter | solution.py:324
  427.6 133.8 %reduce-scatter.23.cloned.1.call-start = ((), (), s32[]{:S(2)}) async-start(), calls=%async_computation.18 | async-start | bytes 5898240 | tf_op jit(solution)/shard_map/reduce_scatter | solution.py:327
  433.3 194.8 %reduce-scatter.27.cloned.1.call-start = ((), (), s32[]{:S(2)}) async-start(), calls=%async_computation.20 | async-start | bytes 884736
  435.5 264.5 %reduce-scatter.25.cloned.1.call-start = ((), (), s32[]{:S(2)}) async-start(), calls=%async_computation.19 | async-start | bytes 2654208
  463.2 309.7 %reduce-scatter.21.cloned.1.call-start = ((), (), s32[]{:S(2)}) async-start(), calls=%async_computation.17 | async-start | bytes 2654208 | tf_op jit(solution)/shard_map/reduce_scatter | solution.py:334
  514.0 331.5 %reduce-scatter.29.cloned.1.call-start = ((), (), s32[]{:S(2)}) async-start(), calls=%async_computation.21 | async-start | bytes 2654208
  (59 other events, 515.7 us)
Sparse Core Ops, SparseCore 0:
  9.5 33.6 all-gather.8
  46.9 44.1 all-gather.10
  93.9 42.5 all-gather.12
  137.9 15.7 all-gather.14
  155.1 37.4 all-gather.16
  194.0 37.4 all-gather.18
  244.8 25.6 reduce-scatter.16
  423.0 37.4 reduce-scatter.14
  463.1 47.9 reduce-scatter.18
  513.4 47.9 reduce-scatter.22
  564.8 63.2 reduce-scatter.26
  631.4 68.5 reduce-scatter.24
  704.1 68.7 reduce-scatter.20
  776.8 68.7 reduce-scatter.28
where the time goes:
time: 853 us; the launch traced here: 852 us
  waiting for transfers between devices  632 us (74%)
  blocking collectives  65 us (8%)
  matrix products  48.1 us (6%)
  local copies, waits for them, and re-layouts  32.4 us (4%)
  other arithmetic  27.2 us (3%)
  starting transfers between devices  25.4 us (3%)
  between operations  15.7 us (2%)
    unnamed x17, waiting for transfers between devices  152 us
    ppermute x32, waiting for transfers between devices, from_behind(): return lax.ppermute(value, axis, pairs)  130 us
    reduce_scatter x1, waiting for transfers between devices, on_device(): lax.psum_scatter(row_sums[2], 'ctx', scatter_dimension=1, tiled=True)  71 us
    unnamed x2, blocking collectives  54.6 us
    reduce_scatter x1, waiting for transfers between devices, on_device(): lax.psum_scatter(matrix_terms[2].astype(jnp.bfloat16), 'fsdp', scatter_di...  47.8 us
    reduce_scatter x1, waiting for transfers between devices, on_device(): lax.psum_scatter(matrix_terms[3].astype(jnp.bfloat16), 'fsdp', scatter_di...  47.4 us
    all_gather x1, waiting for transfers between devices, on_device(): lax.all_gather(values, 'ctx', axis=0, tiled=True)  45.3 us
    all_gather x1, waiting for transfers between devices, on_device(): lax.all_gather(fc_weight, 'fsdp', axis=0, tiled=True)  36.4 us
  transfers between devices with their start and end apart: 46, of which 45 were waited for; matrix products, arithmetic and copies ran while one was open for 10% of the time, Pallas kernels for 0%

commit v1 on v0

--- a/solution.py
+++ b/solution.py
@@ -9,6 +9,16 @@
 epsilon = 1e-05
 negative_big = -1e30
 gelu_coeff = 0.7978845608028654
+
+
+def gather_around(x, axis, dim):
+    ways, here, turn = (lax.axis_size(axis), lax.axis_index(axis), x.shape[dim])
+    dims = [n * ways if d == dim else n for d, n in enumerate(x.shape)]
+    full = lax.dynamic_update_slice_in_dim(jnp.zeros(dims, x.dtype), x, here * turn, axis=dim)
+    for far in range(1, ways):
+        x = lax.ppermute(x, axis, [(d, (d + 1) % ways) for d in range(ways)])
+        full = lax.dynamic_update_slice_in_dim(full, x, (here - far) % ways * turn, axis=dim)
+    return full
 
 
 def from_behind(value, axis, steps):
@@ -207,7 +217,7 @@
     )
     incoming = (
         lax.all_gather(key_rows, "ctx", axis=0, tiled=True),
-        lax.all_gather(values, "ctx", axis=0, tiled=True),
+        gather_around(values, "ctx", 0),
     )
     key_pos = positions_of(block_order, jnp.int32(0), incoming[0].shape[0], block_rows)
     visible = key_pos[None, :] <= own_pos[:, None]

time: 853 us -> 822 us (0.964)
  waiting for transfers between devices: 632 us -> 584 us
  local copies, waits for them, and re-layouts: 32.4 us -> 44.7 us
    ppermute x0 -> x7, waiting for transfers between devices: none -> 65.9 us  [gather_around(): x = lax.ppermute(x, axis, [(d, (d + 1) % ways) for d in range(ways)])]
    all_gather x1 -> x0, waiting for transfers between devices: 45.3 us -> none  [on_device(): lax.all_gather(values, 'ctx', axis=0, tiled=True)]
    all_gather x1, waiting for transfers between devices: 36.4 us -> 0.01 us  [on_device(): lax.all_gather(fc_weight, 'fsdp', axis=0, tiled=True)]
    all_gather x1, waiting for transfers between devices: 27.2 us -> 0.02 us  [on_device(): lax.all_gather(key_rows, 'ctx', axis=0, tiled=True)]
    unnamed x17 -> x16, waiting for transfers between devices: 152 us -> 152 us
    unnamed x108 -> x112, local copies, waits for them, and re-layouts: 27.7 us -> 27.4 us
  transfers between devices with their start and end apart: 46 -> 52, of which waited for: 45 -> 47; matrix products, arithmetic and copies ran while one was open for 10% -> 12% of each run, Pallas kernels for 0% -> 0%
where the time goes in v1:
time: 822 us; the launch traced here: 820 us
  waiting for transfers between devices  584 us (71%)
  blocking collectives  65.1 us (8%)
  matrix products  49 us (6%)
  local copies, waits for them, and re-layouts  44.7 us (5%)
  other arithmetic  28.6 us (3%)
  starting transfers between devices  26.9 us (3%)
  between operations  15.7 us (2%)
    unnamed x16, waiting for transfers between devices  152 us
    ppermute x32, waiting for transfers between devices, from_behind(): return lax.ppermute(value, axis, pairs)  130 us
    reduce_scatter x1, waiting for transfers between devices, on_device(): lax.psum_scatter(row_sums[2], 'ctx', scatter_dimension=1, tiled=True)  71 us
    ppermute x7, waiting for transfers between devices, gather_around(): x = lax.ppermute(x, axis, [(d, (d + 1) % ways) for d in range(ways)])  65.9 us
    unnamed x2, blocking collectives  54.7 us
    reduce_scatter x1, waiting for transfers between devices, on_device(): lax.psum_scatter(matrix_terms[2].astype(jnp.bfloat16), 'fsdp', scatter_di...  47.8 us
    reduce_scatter x1, waiting for transfers between devices, on_device(): lax.psum_scatter(matrix_terms[3].astype(jnp.bfloat16), 'fsdp', scatter_di...  47.5 us
    all_gather x1, waiting for transfers between devices, on_device(): lax.all_gather(down_weight, 'fsdp', axis=0, tiled=True)  32 us
  transfers between devices with their start and end apart: 52, of which 47 were waited for; matrix products, arithmetic and copies ran while one was open for 12% of the time, Pallas kernels for 0%

profile of v1, /device:TPU:0, one launch (start us, length us, event | category | flops | bytes accessed | tf_op | source)
XLA Modules:
  0.0 820.3 jit_solution(10244252191816707935)
XLA Ops:
  14.9 14.1 %all-reduce.15 = (bf16[768]{0:T(1024)(128)(2,1)S(1)}, bf16[768]{0:T(1024)(128)(2,1)S(1)}, bf16[768]{0:T(1024)(128)(2,1)S(1)}, bf16[768]{0:T(1024)(128)(2,1)S(1)}...) all-reduce(bf16[768]{0:T(1024)(128)(2,1)S(1)} %dynamic-update-slice, ...), channel_id=1, replica_groups=mesh['ctx'=8,'fsdp'=4] {'fsdp'}, use_global_device_ids=true, to_apply=%add.1 | all-reduce | flops 4608 | bytes 18432
  31.2 12.0 %all-gather.8.cloned.1.call-done = bf16[768,2304]{1,0:T(8,128)(2,1)} async-done(((bf16[192,2304]{1,0:T(8,128)(2,1)}), bf16[768,2304]{1,0:T(8,128)(2,1)}) %all-gather.8.cloned.1.call-update) | async-done | bytes 3538960 | tf_op jit(solution)/shard_map/all_gather | solution.py:190
  48.8 5.2 all-gather
  55.6 12.6 %collective-permute-done.4 = bf16[128,768]{1,0:T(8,128)(2,1)S(1)} collective-permute-done((bf16[128,768]{1,0:T(8,128)(2,1)S(1)}, bf16[128,768]{1,0:T(8,128)(2,1)S(1)}, u32[]{:S(2)}, u32[]{:S(2)}) %collective-permute-start.4) | collective-permute-done | bytes 196640 | tf_op jit(solution)/shard_map/ppermute | solution.py:19
  68.8 7.7 collective-permute-done.5
  76.7 13.1 %collective-permute-done.6 = bf16[128,768]{1,0:T(8,128)(2,1)S(1)} collective-permute-done((bf16[128,768]{1,0:T(8,128)(2,1)S(1)}, bf16[128,768]{1,0:T(8,128)(2,1)S(1)}, u32[]{:S(2)}, u32[]{:S(2)}) %collective-permute-start.6) | collective-permute-done | bytes 196640 | tf_op jit(solution)/shard_map/ppermute | solution.py:19
  89.9 12.9 %collective-permute-done.7 = bf16[128,768]{1,0:T(8,128)(2,1)S(1)} collective-permute-done((bf16[128,768]{1,0:T(8,128)(2,1)S(1)}, bf16[128,768]{1,0:T(8,128)(2,1)S(1)}, u32[]{:S(2)}, u32[]{:S(2)}) %collective-permute-start.7) | collective-permute-done | bytes 196640 | tf_op jit(solution)/shard_map/ppermute | solution.py:19
  102.8 10.2 %collective-permute-done.8 = bf16[128,768]{1,0:T(8,128)(2,1)S(1)} collective-permute-done((bf16[128,768]{1,0:T(8,128)(2,1)S(1)}, bf16[128,768]{1,0:T(8,128)(2,1)S(1)}, u32[]{:S(2)}, u32[]{:S(2)}) %collective-permute-start.8) | collective-permute-done | bytes 196640 | tf_op jit(solution)/shard_map/ppermute | solution.py:19
  113.0 9.3 %collective-permute-done.9 = bf16[128,768]{1,0:T(8,128)(2,1)S(1)} collective-permute-done((bf16[128,768]{1,0:T(8,128)(2,1)S(1)}, bf16[128,768]{1,0:T(8,128)(2,1)S(1)}, u32[]{:S(2)}, u32[]{:S(2)}) %collective-permute-start.9) | collective-permute-done | bytes 196640 | tf_op jit(solution)/shard_map/ppermute | solution.py:19
  124.5 5.2 all-gather.1
  130.9 27.9 %conditional.2 = (f32[12,128]{1,0:T(8,128)}, f32[12,128]{1,0:T(8,128)}, f32[128,12,64]{0,2,1:T(8,128)S(1)}, f32[12,128]{1,0:T(8,128)S(1)}) conditional(s32[]{:T(128)} %convert_element_type.170, () %tuple.121, (pred[128,1024]{1,0:T(8,128)(4,1)}, bf16[128,768]{1,0:T(8,128)(2,1)S(1)}, bf16[1024,768]{1,0:T(8,128)(2,1)}, s32[]{:T(128)}, ...), branch_computations={%region_5.6_spmd, %region_6.9_spmd.clone.clone} | conditional | flops 423200256 | bytes 69596552 | solution.py:105
  153.0 5.1 fusion.22
  165.9 32.0 %all-gather.16.cloned.1.call-done = bf16[3072,768]{1,0:T(8,128)(2,1)} async-done(((bf16[768,768]{1,0:T(8,128)(2,1)}), bf16[3072,768]{1,0:T(8,128)(2,1)}) %all-gather.16.cloned.1.call-update) | async-done | bytes 4718608 | tf_op jit(solution)/shard_map/all_gather | solution.py:198
  198.0 5.0 fusion.85
  212.0 174.2 %while.25 = (s32[]{:T(128)}, bf16[128,768]{0,1:T(8,128)(2,1)S(1)}, bf16[128,768]{0,1:T(8,128)(2,1)S(1)}, f32[128,12,64]{0,2,1:T(8,128)S(1)}, f32[128,12,64]{0,2,...) while((s32[]{:T(128)}, bf16[128,768]{0,1:T(8,128)(2,1)S(1)}, ...), condition=%wide.region_18.19_spmd.clone, body=%wide.region_13.18_spmd.clone.sunk | while | flops 128329360 | bytes 15188138 | solution.py:293
  221.5 4.5 collective-permute-done.2
  243.8 6.3 collective-permute-done.2
  250.1 4.2 collective-permute-done.3
  267.0 8.1 collective-permute-done.2
  288.3 9.2 %collective-permute-done.2 = bf16[128,12,64]{0,2,1:T(8,128)(2,1)S(1)} collective-permute-done((bf16[128,12,64]{0,2,1:T(8,128)(2,1)S(1)}, bf16[128,12,64]{0,2,1:T(8,128)(2,1)S(1)}, u32[]{:S(2)}, u32[]{:S(2)}) %collective-permute-start.2) | collective-permute-done | bytes 196640 | tf_op jit(solution)/shard_map/while/body/eval_jaxpr/ppermute | solution.py:27
  310.3 8.7 %collective-permute-done.2 = bf16[128,12,64]{0,2,1:T(8,128)(2,1)S(1)} collective-permute-done((bf16[128,12,64]{0,2,1:T(8,128)(2,1)S(1)}, bf16[128,12,64]{0,2,1:T(8,128)(2,1)S(1)}, u32[]{:S(2)}, u32[]{:S(2)}) %collective-permute-start.2) | collective-permute-done | bytes 196640 | tf_op jit(solution)/shard_map/while/body/eval_jaxpr/ppermute | solution.py:27
  332.2 7.5 collective-permute-done.2
  353.3 8.1 collective-permute-done.2
  373.5 6.4 collective-permute-done.2
  402.9 25.1 %reduce-scatter.15.cloned.1.call-done = bf16[192,2304]{1,0:T(8,128)(2,1)} async-done(((bf16[768,2304]{1,0:T(8,128)(2,1)}), bf16[192,2304]{1,0:T(8,128)(2,1)}) %reduce-scatter.15.cloned.1.call-update) | async-done | bytes 884752 | tf_op jit(solution)/shard_map/reduce_scatter | solution.py:328
  430.7 47.8 %reduce-scatter.19.cloned.1.call-done = bf16[192,3072]{1,0:T(8,128)(2,1)} async-done(((bf16[768,3072]{1,0:T(8,128)(2,1)}), bf16[192,3072]{1,0:T(8,128)(2,1)}) %reduce-scatter.19.cloned.1.call-update) | async-done | bytes 1179664 | tf_op jit(solution)/shard_map/reduce_scatter | solution.py:334
  481.5 47.5 %reduce-scatter.23.cloned.1.call-done = bf16[768,768]{1,0:T(8,128)(2,1)} async-done(((bf16[3072,768]{1,0:T(8,128)(2,1)}), bf16[768,768]{1,0:T(8,128)(2,1)}) %reduce-scatter.23.cloned.1.call-update) | async-done | bytes 1179664 | tf_op jit(solution)/shard_map/reduce_scatter | solution.py:337
  537.2 40.6 %all-reduce.14 = (f32[768]{0:T(1024)S(1)}, f32[768]{0:T(1024)S(1)}, f32[1536]{0:T(1024)S(1)}, f32[768]{0:T(1024)S(1)}, f32[768]{0:T(1024)S(1)}, /*index=5*/f32[7...) all-reduce(f32[768]{0:T(1024)} %get-tuple-element.1428, ...), channel_id=2, replica_groups=mesh['ctx'=8,'fsdp'=4] {'ctx','fsdp'}, use_global_device_ids=true, to_apply=%region_22.23.clone | all-reduce | flops 9216 | bytes 73728
  589.5 6.2 reduce-scatter.27.cloned.1.call-done
  597.4 70.7 %reduce-scatter.25.cloned.1.call-done = f32[288,192]{1,0:T(8,128)} async-done(((f32[2304,192]{1,0:T(8,128)}), f32[288,192]{1,0:T(8,128)}) %reduce-scatter.25.cloned.1.call-update) | async-done | bytes 221200
  669.8 71.0 %reduce-scatter.21.cloned.1.call-done = f32[192,384]{1,0:T(8,128)} async-done(((f32[192,3072]{1,0:T(8,128)}), f32[192,384]{1,0:T(8,128)}) %reduce-scatter.21.cloned.1.call-update) | async-done | bytes 294928 | tf_op jit(solution)/shard_map/reduce_scatter | solution.py:344
  740.8 73.0 %reduce-scatter.29.cloned.1.call-done = f32[96,768]{1,0:T(8,128)} async-done(((f32[768,768]{1,0:T(8,128)}), f32[96,768]{1,0:T(8,128)}) %reduce-scatter.29.cloned.1.call-update) | async-done | bytes 294928
  (408 shorter events, 214.1 us)
Async XLA Ops:
  7.2 36.0 %all-gather.8.cloned.1.call-start = ((), (), s32[]{:S(2)}) async-start(), calls=%async_computation.8 | async-start | bytes 4423680 | tf_op jit(solution)/shard_map/all_gather | solution.py:190
  7.9 122.9 %all-gather.10.cloned.1.call-start = ((), (), s32[]{:S(2)}) async-start(), calls=%async_computation.9 | async-start | bytes 1769472 | tf_op jit(solution)/shard_map/all_gather | solution.py:219
  46.8 113.4 %all-gather.12.cloned.1.call-start = ((), (), s32[]{:S(2)}) async-start(), calls=%async_computation.10 | async-start | bytes 1474560 | tf_op jit(solution)/shard_map/all_gather | solution.py:192
  47.5 115.1 %all-gather.14.cloned.1.call-start = ((), (), s32[]{:S(2)}) async-start(), calls=%async_computation.11 | async-start | bytes 5898240 | tf_op jit(solution)/shard_map/all_gather | solution.py:196
  48.1 149.8 %all-gather.16.cloned.1.call-start = ((), (), s32[]{:S(2)}) async-start(), calls=%async_computation.12 | async-start | bytes 5898240 | tf_op jit(solution)/shard_map/all_gather | solution.py:198
  48.7 352.0 %reduce-scatter.17.cloned.1.call-start = ((), (), s32[]{:S(2)}) async-start(), calls=%async_computation.14 | async-start | bytes 1474560 | tf_op jit(solution)/shard_map/reduce_scatter | solution.py:331
  211.2 216.7 %reduce-scatter.15.cloned.1.call-start = ((), (), s32[]{:S(2)}) async-start(), calls=%async_computation.13 | async-start | bytes 4423680 | tf_op jit(solution)/shard_map/reduce_scatter | solution.py:328
  218.6 15.9 %collective-permute-start = (bf16[128,768]{0,1:T(8,128)(2,1)S(1)}, bf16[128,768]{0,1:T(8,128)(2,1)S(1)}, u32[]{:S(2)}, u32[]{:S(2)}) collective-permute-start(bf16[128,768]{0,1:T(8,128)(2,1)S(1)} %copy.149), channel_id=1, source_target_pairs={{0,4},{4,8},{8,12},{12,16},{16,20},{20,24},{24,28},{28,0},{1,5},{5... | collective-permute-start | bytes 589832 | tf_op jit(solution)/shard_map/while/body/eval_jaxpr/ppermute | solution.py:27
  220.0 17.9 %collective-permute-start.1 = (bf16[128,768]{0,1:T(8,128)(2,1)S(1)}, bf16[128,768]{0,1:T(8,128)(2,1)S(1)}, u32[]{:S(2)}, u32[]{:S(2)}) collective-permute-start(bf16[128,768]{0,1:T(8,128)(2,1)S(1)} %copy.150), channel_id=1, source_target_pairs={{0,4},{4,8},{8,12},{12,16},{16,20},{20,24},{24,28},{28,0},{1,5},{5... | collective-permute-start | bytes 589832 | tf_op jit(solution)/shard_map/while/body/eval_jaxpr/ppermute | solution.py:27
  242.6 15.9 %collective-permute-start = (bf16[128,768]{0,1:T(8,128)(2,1)S(1)}, bf16[128,768]{0,1:T(8,128)(2,1)S(1)}, u32[]{:S(2)}, u32[]{:S(2)}) collective-permute-start(bf16[128,768]{0,1:T(8,128)(2,1)S(1)} %copy.149), channel_id=1, source_target_pairs={{0,4},{4,8},{8,12},{12,16},{16,20},{20,24},{24,28},{28,0},{1,5},{5... | collective-permute-start | bytes 589832 | tf_op jit(solution)/shard_map/while/body/eval_jaxpr/ppermute | solution.py:27
  243.2 18.0 %collective-permute-start.1 = (bf16[128,768]{0,1:T(8,128)(2,1)S(1)}, bf16[128,768]{0,1:T(8,128)(2,1)S(1)}, u32[]{:S(2)}, u32[]{:S(2)}) collective-permute-start(bf16[128,768]{0,1:T(8,128)(2,1)S(1)} %copy.150), channel_id=1, source_target_pairs={{0,4},{4,8},{8,12},{12,16},{16,20},{20,24},{24,28},{28,0},{1,5},{5... | collective-permute-start | bytes 589832 | tf_op jit(solution)/shard_map/while/body/eval_jaxpr/ppermute | solution.py:27
  264.7 14.6 %collective-permute-start.3 = (bf16[128,12,64]{0,2,1:T(8,128)(2,1)S(1)}, bf16[128,12,64]{0,2,1:T(8,128)(2,1)S(1)}, u32[]{:S(2)}, u32[]{:S(2)}) collective-permute-start(bf16[128,12,64]{0,2,1:T(8,128)(2,1)S(1)} %convert_element_type.306), channel_id=1, source_target_pairs={{0,4},{4,8},{8,12},{12,16},{16,20},{20,24},{24,28},{28,0},{1,5},{5... | collective-permute-start | bytes 589832 | tf_op jit(solution)/shard_map/while/body/eval_jaxpr/ppermute | solution.py:27
  265.8 17.4 %collective-permute-start = (bf16[128,768]{0,1:T(8,128)(2,1)S(1)}, bf16[128,768]{0,1:T(8,128)(2,1)S(1)}, u32[]{:S(2)}, u32[]{:S(2)}) collective-permute-start(bf16[128,768]{0,1:T(8,128)(2,1)S(1)} %copy.149), channel_id=1, source_target_pairs={{0,4},{4,8},{8,12},{12,16},{16,20},{20,24},{24,28},{28,0},{1,5},{5... | collective-permute-start | bytes 589832 | tf_op jit(solution)/shard_map/while/body/eval_jaxpr/ppermute | solution.py:27
  265.9 19.4 %collective-permute-start.1 = (bf16[128,768]{0,1:T(8,128)(2,1)S(1)}, bf16[128,768]{0,1:T(8,128)(2,1)S(1)}, u32[]{:S(2)}, u32[]{:S(2)}) collective-permute-start(bf16[128,768]{0,1:T(8,128)(2,1)S(1)} %copy.150), channel_id=1, source_target_pairs={{0,4},{4,8},{8,12},{12,16},{16,20},{20,24},{24,28},{28,0},{1,5},{5... | collective-permute-start | bytes 589832 | tf_op jit(solution)/shard_map/while/body/eval_jaxpr/ppermute | solution.py:27
  287.1 14.6 %collective-permute-start.3 = (bf16[128,12,64]{0,2,1:T(8,128)(2,1)S(1)}, bf16[128,12,64]{0,2,1:T(8,128)(2,1)S(1)}, u32[]{:S(2)}, u32[]{:S(2)}) collective-permute-start(bf16[128,12,64]{0,2,1:T(8,128)(2,1)S(1)} %convert_element_type.306), channel_id=1, source_target_pairs={{0,4},{4,8},{8,12},{12,16},{16,20},{20,24},{24,28},{28,0},{1,5},{5... | collective-permute-start | bytes 589832 | tf_op jit(solution)/shard_map/while/body/eval_jaxpr/ppermute | solution.py:27
  288.2 16.6 %collective-permute-start = (bf16[128,768]{0,1:T(8,128)(2,1)S(1)}, bf16[128,768]{0,1:T(8,128)(2,1)S(1)}, u32[]{:S(2)}, u32[]{:S(2)}) collective-permute-start(bf16[128,768]{0,1:T(8,128)(2,1)S(1)} %copy.149), channel_id=1, source_target_pairs={{0,4},{4,8},{8,12},{12,16},{16,20},{20,24},{24,28},{28,0},{1,5},{5... | collective-permute-start | bytes 589832 | tf_op jit(solution)/shard_map/while/body/eval_jaxpr/ppermute | solution.py:27
  288.2 18.6 %collective-permute-start.1 = (bf16[128,768]{0,1:T(8,128)(2,1)S(1)}, bf16[128,768]{0,1:T(8,128)(2,1)S(1)}, u32[]{:S(2)}, u32[]{:S(2)}) collective-permute-start(bf16[128,768]{0,1:T(8,128)(2,1)S(1)} %copy.150), channel_id=1, source_target_pairs={{0,4},{4,8},{8,12},{12,16},{16,20},{20,24},{24,28},{28,0},{1,5},{5... | collective-permute-start | bytes 589832 | tf_op jit(solution)/shard_map/while/body/eval_jaxpr/ppermute | solution.py:27
  308.6 14.6 %collective-permute-start.3 = (bf16[128,12,64]{0,2,1:T(8,128)(2,1)S(1)}, bf16[128,12,64]{0,2,1:T(8,128)(2,1)S(1)}, u32[]{:S(2)}, u32[]{:S(2)}) collective-permute-start(bf16[128,12,64]{0,2,1:T(8,128)(2,1)S(1)} %convert_element_type.306), channel_id=1, source_target_pairs={{0,4},{4,8},{8,12},{12,16},{16,20},{20,24},{24,28},{28,0},{1,5},{5... | collective-permute-start | bytes 589832 | tf_op jit(solution)/shard_map/while/body/eval_jaxpr/ppermute | solution.py:27
  309.7 15.8 %collective-permute-start = (bf16[128,768]{0,1:T(8,128)(2,1)S(1)}, bf16[128,768]{0,1:T(8,128)(2,1)S(1)}, u32[]{:S(2)}, u32[]{:S(2)}) collective-permute-start(bf16[128,768]{0,1:T(8,128)(2,1)S(1)} %copy.149), channel_id=1, source_target_pairs={{0,4},{4,8},{8,12},{12,16},{16,20},{20,24},{24,28},{28,0},{1,5},{5... | collective-permute-start | bytes 589832 | tf_op jit(solution)/shard_map/while/body/eval_jaxpr/ppermute | solution.py:27
  309.7 17.8 %collective-permute-start.1 = (bf16[128,768]{0,1:T(8,128)(2,1)S(1)}, bf16[128,768]{0,1:T(8,128)(2,1)S(1)}, u32[]{:S(2)}, u32[]{:S(2)}) collective-permute-start(bf16[128,768]{0,1:T(8,128)(2,1)S(1)} %copy.150), channel_id=1, source_target_pairs={{0,4},{4,8},{8,12},{12,16},{16,20},{20,24},{24,28},{28,0},{1,5},{5... | collective-permute-start | bytes 589832 | tf_op jit(solution)/shard_map/while/body/eval_jaxpr/ppermute | solution.py:27
  330.3 15.0 %collective-permute-start = (bf16[128,768]{0,1:T(8,128)(2,1)S(1)}, bf16[128,768]{0,1:T(8,128)(2,1)S(1)}, u32[]{:S(2)}, u32[]{:S(2)}) collective-permute-start(bf16[128,768]{0,1:T(8,128)(2,1)S(1)} %copy.149), channel_id=1, source_target_pairs={{0,4},{4,8},{8,12},{12,16},{16,20},{20,24},{24,28},{28,0},{1,5},{5... | collective-permute-start | bytes 589832 | tf_op jit(solution)/shard_map/while/body/eval_jaxpr/ppermute | solution.py:27
  330.4 17.0 %collective-permute-start.1 = (bf16[128,768]{0,1:T(8,128)(2,1)S(1)}, bf16[128,768]{0,1:T(8,128)(2,1)S(1)}, u32[]{:S(2)}, u32[]{:S(2)}) collective-permute-start(bf16[128,768]{0,1:T(8,128)(2,1)S(1)} %copy.150), channel_id=1, source_target_pairs={{0,4},{4,8},{8,12},{12,16},{16,20},{20,24},{24,28},{28,0},{1,5},{5... | collective-permute-start | bytes 589832 | tf_op jit(solution)/shard_map/while/body/eval_jaxpr/ppermute | solution.py:27
  351.0 15.0 %collective-permute-start = (bf16[128,768]{0,1:T(8,128)(2,1)S(1)}, bf16[128,768]{0,1:T(8,128)(2,1)S(1)}, u32[]{:S(2)}, u32[]{:S(2)}) collective-permute-start(bf16[128,768]{0,1:T(8,128)(2,1)S(1)} %copy.149), channel_id=1, source_target_pairs={{0,4},{4,8},{8,12},{12,16},{16,20},{20,24},{24,28},{28,0},{1,5},{5... | collective-permute-start | bytes 589832 | tf_op jit(solution)/shard_map/while/body/eval_jaxpr/ppermute | solution.py:27
  351.0 17.1 %collective-permute-start.1 = (bf16[128,768]{0,1:T(8,128)(2,1)S(1)}, bf16[128,768]{0,1:T(8,128)(2,1)S(1)}, u32[]{:S(2)}, u32[]{:S(2)}) collective-permute-start(bf16[128,768]{0,1:T(8,128)(2,1)S(1)} %copy.150), channel_id=1, source_target_pairs={{0,4},{4,8},{8,12},{12,16},{16,20},{20,24},{24,28},{28,0},{1,5},{5... | collective-permute-start | bytes 589832 | tf_op jit(solution)/shard_map/while/body/eval_jaxpr/ppermute | solution.py:27
  370.0 14.2 %collective-permute-start = (bf16[128,768]{0,1:T(8,128)(2,1)S(1)}, bf16[128,768]{0,1:T(8,128)(2,1)S(1)}, u32[]{:S(2)}, u32[]{:S(2)}) collective-permute-start(bf16[128,768]{0,1:T(8,128)(2,1)S(1)} %copy.149), channel_id=1, source_target_pairs={{0,4},{4,8},{8,12},{12,16},{16,20},{20,24},{24,28},{28,0},{1,5},{5... | collective-permute-start | bytes 589832 | tf_op jit(solution)/shard_map/while/body/eval_jaxpr/ppermute | solution.py:27
  370.3 16.0 %collective-permute-start.1 = (bf16[128,768]{0,1:T(8,128)(2,1)S(1)}, bf16[128,768]{0,1:T(8,128)(2,1)S(1)}, u32[]{:S(2)}, u32[]{:S(2)}) collective-permute-start(bf16[128,768]{0,1:T(8,128)(2,1)S(1)} %copy.150), channel_id=1, source_target_pairs={{0,4},{4,8},{8,12},{12,16},{16,20},{20,24},{24,28},{28,0},{1,5},{5... | collective-permute-start | bytes 589832 | tf_op jit(solution)/shard_map/while/body/eval_jaxpr/ppermute | solution.py:27
  390.3 88.2 %reduce-scatter.19.cloned.1.call-start = ((), (), s32[]{:S(2)}) async-start(), calls=%async_computation.15 | async-start | bytes 5898240 | tf_op jit(solution)/shard_map/reduce_scatter | solution.py:334
  395.0 134.0 %reduce-scatter.23.cloned.1.call-start = ((), (), s32[]{:S(2)}) async-start(), calls=%async_computation.17 | async-start | bytes 5898240 | tf_op jit(solution)/shard_map/reduce_scatter | solution.py:337
  400.7 195.0 %reduce-scatter.27.cloned.1.call-start = ((), (), s32[]{:S(2)}) async-start(), calls=%async_computation.19 | async-start | bytes 884736
  402.8 265.2 %reduce-scatter.25.cloned.1.call-start = ((), (), s32[]{:S(2)}) async-start(), calls=%async_computation.18 | async-start | bytes 2654208
  430.6 310.2 %reduce-scatter.21.cloned.1.call-start = ((), (), s32[]{:S(2)}) async-start(), calls=%async_computation.16 | async-start | bytes 2654208 | tf_op jit(solution)/shard_map/reduce_scatter | solution.py:344
  481.4 332.4 %reduce-scatter.29.cloned.1.call-start = ((), (), s32[]{:S(2)}) async-start(), calls=%async_computation.20 | async-start | bytes 2654208
  (67 other events, 836.6 us)
Sparse Core Ops, SparseCore 0:
  9.5 33.6 all-gather.7
  46.9 53.3 all-gather.9
  101.8 18.3 all-gather.11
  121.6 37.4 all-gather.13
  160.5 37.4 all-gather.15
  211.3 25.5 reduce-scatter.16
  390.4 37.4 reduce-scatter.14
  430.4 47.9 reduce-scatter.18
  481.0 47.9 reduce-scatter.22
  532.1 63.5 reduce-scatter.26
  599.2 68.7 reduce-scatter.24
  671.9 68.8 reduce-scatter.20
  744.9 68.8 reduce-scatter.28
